TPU v7x, 1024 devices: a whole 8x8x8 slice. The times are simulated.
1024 devices in a mesh: layer: 256 (over y, z_hi, x), dp: 4 (over z_lo, core).
Axes of the slice: x: 8, y: 8, z: 8 (z_hi: 4, z_lo: 2; z = z_hi * 2 + z_lo), core: 2. Of those that a mesh axis runs over, the one named last changes fastest.
Arguments:
- activations: bfloat16 [256, 512, 8192], P('layer', 'dp'), may hold values from -6 to 6
- gradients: bfloat16 [256, 512, 896], P('layer', 'dp'), may hold values from -6 to 6
- input_factor: bfloat16 [256, 8192, 256], P('layer', 'dp'), may hold values from -0.0625 to 0.0625
- output_factor: bfloat16 [256, 896, 256], P('layer', 'dp'), may hold values from -0.1875 to 0.1875
- lengths: int32 [16], P('dp'), may hold values from 1 to 32, 320 in all
Outputs:
- influence: float32 [16, 8], P('dp')
Inputs may be any that keep to these rules, and one draw needn't show every extreme that they name: `lengths`: each sequence's live tokens fill the front of its slots; the counts sum to 320 and one sequence fills all 32 slots.
All inputs are finite; a program needn't handle non-finite values. No bound on the sum of `lengths` on one device may be relied on, other than what follows from the above.
Results may differ from a plain program's by a relative error of at most 0.0003.
Values may be sent and summed in bfloat16 or wider, within the bound.
A program may use at most 32 MiB of HBM per device.

v0:
```python
import math

import jax
import jax.numpy as jnp
from jax import lax
from jax.sharding import PartitionSpec as P

RANK = 32
QUERIES = 8
SLOT = 32


def live_tokens(lengths, count):
    position = jnp.arange(count, dtype=jnp.int32)
    sequence = position // SLOT
    owners = sequence[:, None] == jnp.arange(lengths.shape[0], dtype=jnp.int32)[None, :]
    limit = jnp.sum(jnp.where(owners, lengths[None, :], 0), axis=1)
    return (position % SLOT < limit).astype(jnp.float32)


def rank_sum(first, second):
    return jnp.sum((first * second).reshape(first.shape[0], QUERIES, RANK), axis=2)


def shards(activations, gradients, input_factor, output_factor, lengths):
    tokens = activations.shape[1]
    act_rows = activations[0]
    columns = act_rows
    projected_in = jnp.dot(
        columns,
        lax.all_gather(input_factor, "dp", axis=1, tiled=True)[0],
        preferred_element_type=jnp.float32,
    )
    grad_rows = gradients[0]
    columns = grad_rows
    projected_out = jnp.dot(
        columns,
        lax.all_gather(output_factor, "dp", axis=1, tiled=True)[0],
        preferred_element_type=jnp.float32,
    )
    token_score = rank_sum(projected_out, projected_in)
    live = live_tokens(lengths, tokens)
    per_sequence = jnp.sum(
        (token_score * live[:, None]).reshape(lengths.shape[0], SLOT, QUERIES), axis=1
    )
    summed = lax.psum(per_sequence, "layer")
    blocks = lax.axis_size("layer")
    return summed / jnp.float32(math.sqrt(RANK * SLOT * blocks))


def solution(mesh):
    in_specs = (
        P("layer", "dp", None),
        P("layer", "dp", None),
        P("layer", "dp", None),
        P("layer", "dp", None),
        P("dp"),
    )
    out_specs = P("dp", None)
    return jax.shard_map(shards, mesh=mesh, in_specs=in_specs, out_specs=out_specs, check_vma=False)
```

profile of v0, /device:TPU:128, one launch (start us, length us, event | category | flops | bytes accessed | tf_op | source)
XLA Modules:
  0.0 834.4 jit_solution(9434738349455655104)
XLA Ops:
  6.5 0.0 copy-start
  6.5 0.0 copy-start.1
  6.5 0.0 all-gather.2.cloned.1.call-start
  6.5 0.7 all-gather.2.cloned.1.call-update
  7.3 0.7 select_reduce_fusion
  8.0 0.1 reduce_sum.34
  8.1 16.9 %all_gather.6 = bf16[1,896,256]{2,1,0:T(8,128)(2,1)S(1)} all-gather(bf16[1,224,256]{2,1,0:T(8,128)(2,1)} %param.8), channel_id=1, replica_groups=mesh['layer'=256,'dp'=4] {'dp'}, dimensions={1}, use_global_device_ids=true | all-gather | bytes 573440 | tf_op jit(solution)/shard_map/all_gather | solution.py:38
  25.0 47.7 %all-gather.2.cloned.1.call-done = bf16[1,8192,256]{2,1,0:T(8,128)(2,1)} async-done(((bf16[1,2048,256]{2,1,0:T(8,128)(2,1)}), bf16[1,8192,256]{2,1,0:T(8,128)(2,1)}) %all-gather.2.cloned.1.call-update) | async-done | bytes 4194320 | tf_op jit(solution)/shard_map/all_gather | solution.py:31
  72.7 0.0 copy-done
  72.7 2.9 fusion
  75.6 0.0 copy-done.1
  75.6 0.2 convolution_multiply_fusion
  75.8 0.1 copy.10
  76.0 0.1 reduce_sum.32
  76.1 0.1 multiply_reduce_fusion
  76.1 750.7 %psum.7 = f32[4,8]{0,1:T(8,128)S(1)} all-reduce(f32[4,8]{0,1:T(8,128)S(1)} %multiply_reduce_fusion), channel_id=1, replica_groups=mesh['layer'=256,'dp'=4] {'layer'}, use_global_device_ids=true, to_apply=%region_3.4 | all-reduce | flops 32 | bytes 256 | tf_op jit(solution)/shard_map/psum | solution.py:46
  826.9 0.7 copy.11
  (4 shorter events, 0.0 us)
Async XLA Ops:
  6.5 66.2 %copy-start = (bf16[1,128,8192]{2,1,0:T(8,128)(2,1)S(1)}, bf16[1,128,8192]{2,1,0:T(8,128)(2,1)}, u32[]{:S(2)}) copy-start(bf16[1,128,8192]{2,1,0:T(8,128)(2,1)} %param.5) | copy-start | bytes 6291460
  6.5 69.1 %copy-start.1 = (bf16[1,128,896]{2,1,0:T(8,128)(2,1)S(1)}, bf16[1,128,896]{2,1,0:T(8,128)(2,1)}, u32[]{:S(2)}) copy-start(bf16[1,128,896]{2,1,0:T(8,128)(2,1)} %param.6) | copy-start | bytes 688132
  6.5 66.1 %all-gather.2.cloned.1.call-start = ((), (), s32[]{:S(2)}) async-start(), calls=%async_computation | async-start | bytes 5242880 | tf_op jit(solution)/shard_map/all_gather | solution.py:31
Sparse Core Ops, SparseCore 0:
  10.0 62.6 all-gather.1
where the time goes:
time: 835 us; the launch traced here: 834 us
  blocking collectives  768 us (92%)
  waiting for transfers between devices  48.4 us (6%)
  between operations  13.4 us (2%)
    psum x1, blocking collectives, shards(): summed = lax.psum(per_sequence, 'layer')  751 us
    all_gather x1, waiting for transfers between devices, shards(): lax.all_gather(input_factor, 'dp', axis=1, tiled=True)[0]  47.7 us
    all_gather x1, blocking collectives, shards(): lax.all_gather(output_factor, 'dp', axis=1, tiled=True)[0]  16.9 us
  transfers between devices with their start and end apart: 1, of which 1 were waited for; matrix products, arithmetic and copies ran while one was open for 0% of the time, Pallas kernels for 0%

commit v1 on v0

v1 whole, which is shorter than its diff:
```python
import functools
import math

import jax
import jax.numpy as jnp
from jax import lax
from jax.experimental import pallas as pl
from jax.experimental.pallas import tpu as pltpu
from jax.sharding import PartitionSpec as P

RANK = 32
QUERIES = 8
SLOT = 32
LANES = 128
MESH = pl.DeviceIdType.MESH
LAYER_DIMS = {256: (8, 4, 8), 8: (2, 2, 2), 4: (2, 1, 2)}
CHUNKS = 8


def kernel(
    dims, blocks, act, grad, inf, outf, lens, out,
    act_v, grad_v, of_v, if_v, len_v, pi, po, rx1, rx2, rx3,
    local_sem, out_send, out_recv, core_send, core_recv, if_send, if_recv,
    send1, recv1, send2, recv2, send3, recv3,
):
    ny, nz, nx = dims
    layer, dp = lax.axis_index("layer"), lax.axis_index("dp")
    x = lax.rem(layer, nx)
    z = lax.rem(layer // nx, nz)
    y = layer // (nx * nz)
    core = lax.rem(dp, 2)
    chip = dp // 2
    partner = chip * 2 + 1 - core
    cross = (1 - chip) * 2 + core
    tokens, depth = act.shape[1], inf.shape[1]
    odepth = outf.shape[1]
    step = depth // CHUNKS

    def at(y_, z_, x_):
        return (y_ * nz + z_) * nx + x_

    first = [(d, o) for o in (0, 1) for d in range(nx) if d or o]

    def peer1(d, o):
        c = core if o == 0 else 1 - core
        return {"layer": at(y, z, lax.rem(x + d, nx)), "dp": chip * 2 + c}

    def peer2(d):
        return {"layer": at(lax.rem(y + d, ny), z, x), "dp": dp}

    def peer3(d):
        return {"layer": at(y, lax.rem(z + d, nz), x), "dp": dp}

    barrier = pltpu.get_barrier_semaphore()
    peers = [{"layer": layer, "dp": cross}]
    peers += [peer1(d, o) for d, o in first]
    peers += [peer2(d) for d in range(1, ny)]
    peers += [peer3(d) for d in range(1, nz)]
    for peer in peers:
        pl.semaphore_signal(barrier, inc=1, device_id=peer, device_id_type=MESH)

    def columns(shard):
        return pl.ds(pl.multiple_of(shard * depth, LANES), depth)

    mine = pl.ds(pl.multiple_of(core * tokens, 128), tokens)
    local = [
        pltpu.make_async_copy(act.at[0, :, columns(dp)], act_v.at[0, mine, :], local_sem.at[0]),
        pltpu.make_async_copy(act.at[0, :, columns(cross)], act_v.at[1, mine, :], local_sem.at[1]),
        pltpu.make_async_copy(grad.at[0], grad_v.at[mine, :], local_sem.at[2]),
        pltpu.make_async_copy(inf.at[0], if_v.at[0], local_sem.at[3]),
        pltpu.make_async_copy(outf.at[0], of_v.at[dp], local_sem.at[4]),
        pltpu.make_async_copy(lens, len_v.at[core], local_sem.at[5]),
    ]
    for copy in local:
        copy.start()
    pl.semaphore_wait(barrier, len(peers))

    def remote(src, dst, send, recv, device):
        return pltpu.make_async_remote_copy(
            src_ref=src, dst_ref=dst, send_sem=send, recv_sem=recv, device_id=device, device_id_type=MESH
        )

    over = {"layer": layer, "dp": cross}
    beside = {"layer": layer, "dp": partner}
    out_over = remote(outf.at[0], of_v.at[dp], out_send, out_recv, over)
    out_over.start()

    def chunk(i):
        rows = pl.ds(pl.multiple_of(i * step, 16), step)
        return remote(inf.at[0, rows, :], if_v.at[1, rows, :], if_send.at[i], if_recv.at[i], over)

    for i in range(CHUNKS):
        chunk(i).start()

    partner_cross = (1 - chip) * 2 + 1 - core
    swaps = [
        remote(lens, len_v.at[core], core_send.at[0], core_recv.at[0], beside),
        remote(outf.at[0], of_v.at[dp], core_send.at[1], core_recv.at[1], beside),
        remote(grad.at[0], grad_v.at[mine, :], core_send.at[2], core_recv.at[2], beside),
        remote(act.at[0, :, columns(partner)], act_v.at[0, mine, :], core_send.at[3], core_recv.at[3], beside),
        remote(act.at[0, :, columns(partner_cross)], act_v.at[1, mine, :], core_send.at[4], core_recv.at[4], beside),
    ]
    for copy in swaps:
        copy.start()
    relay = remote(of_v.at[cross], of_v.at[cross], core_send.at[5], core_recv.at[5], beside)

    for copy in local:
        copy.wait()
    for copy in swaps:
        copy.wait()

    def contract(block):
        def body(i, carry):
            rows = pl.ds(pl.multiple_of(i * step, LANES), step)
            if block == 1:
                chunk(i).wait()
            product = jnp.dot(act_v[block, :, rows], if_v[block, rows, :], preferred_element_type=jnp.float32)
            if block == 0:
                pi[...] = jnp.where(i == 0, product, pi[...] + product)
            else:
                pi[...] += product
            return carry

        lax.fori_loop(0, CHUNKS, body, 0)

    out_over.wait()
    relay.start()
    pi[...] = jnp.zeros_like(pi)
    contract(0)
    relay.wait()

    seqs = tokens // SLOT
    row = lax.broadcasted_iota(jnp.int32, (2 * tokens, 1), 0)
    limit = jnp.zeros((2 * tokens, 1), jnp.int32)
    for s in range(2 * seqs):
        count = len_v[s // seqs][:, s % seqs : s % seqs + 1]
        limit = jnp.where(row // SLOT == s, count, limit)
    live = (row % SLOT < limit).astype(jnp.float32)
    total = jnp.zeros(po.shape, jnp.float32)
    for shard in range(4):
        total += jnp.dot(
            grad_v[:, shard * odepth : (shard + 1) * odepth], of_v[shard], preferred_element_type=jnp.float32
        )
    po[...] = total * live
    contract(1)

    width = QUERIES * RANK
    lanes = lax.broadcasted_iota(jnp.int32, (width, LANES), 1)
    fold = (lax.broadcasted_iota(jnp.int32, (width, LANES), 0) // RANK == lanes % QUERIES).astype(jnp.float32)
    score = jnp.sum((po[...] * pi[...]).reshape(2 * seqs, SLOT, width), axis=1)
    score = jnp.dot(score, fold, precision=lax.Precision.HIGHEST, preferred_element_type=jnp.float32)
    spot = lax.broadcasted_iota(jnp.int32, (2 * seqs, LANES), 1) // QUERIES
    keep = spot == lax.broadcasted_iota(jnp.int32, (2 * seqs, LANES), 0)
    value = jnp.sum(jnp.where(keep, score, 0.0), axis=0, keepdims=True)

    def exchange(value, rx, me, sends):
        rx[me] = value
        copies = [remote(rx.at[me], rx.at[me], s, r, device) for s, r, device in sends]
        for copy in copies:
            copy.start()
        for copy in copies:
            copy.wait()
        result = rx[0]
        for j in range(1, rx.shape[0]):
            result = result + rx[j]
        return result

    value = exchange(
        value, rx1, core * nx + x, [(send1.at[i], recv1.at[i], peer1(d, o)) for i, (d, o) in enumerate(first)]
    )
    value = exchange(value, rx2, y, [(send2.at[d], recv2.at[d], peer2(d)) for d in range(1, ny)])
    if nz > 1:
        value = exchange(value, rx3, z, [(send3.at[d], recv3.at[d], peer3(d)) for d in range(1, nz)])

    own = lax.broadcasted_iota(jnp.int32, (8, LANES), 0) + core * seqs
    lane = lax.broadcasted_iota(jnp.int32, (8, LANES), 1)
    spread = jnp.where(lane // QUERIES == own, jnp.broadcast_to(value, (8, LANES)), 0.0)
    gather = (
        lax.broadcasted_iota(jnp.int32, (LANES, LANES), 0) % QUERIES
        == lax.broadcasted_iota(jnp.int32, (LANES, LANES), 1)
    ).astype(jnp.float32)
    final = jnp.dot(spread, gather, precision=lax.Precision.HIGHEST, preferred_element_type=jnp.float32)
    out[...] = final[:seqs, :QUERIES] / jnp.float32(math.sqrt(RANK * SLOT * blocks))


def shards(activations, gradients, input_factor, output_factor, lengths):
    blocks = lax.axis_size("layer")
    dims = LAYER_DIMS[blocks]
    ny, nz, nx = dims
    tokens = activations.shape[1]
    depth, width = input_factor.shape[1:]
    odepth = output_factor.shape[1]
    seqs = lengths.shape[0]
    bf16, f32 = jnp.bfloat16, jnp.float32
    dma = pltpu.SemaphoreType.DMA
    anywhere = pl.BlockSpec(memory_space=pl.ANY)
    return pl.pallas_call(
        functools.partial(kernel, dims, blocks),
        out_shape=jax.ShapeDtypeStruct((seqs, QUERIES), f32),
        in_specs=[anywhere] * 5,
        out_specs=pl.BlockSpec(memory_space=pltpu.VMEM),
        scratch_shapes=[
            pltpu.VMEM((2, 2 * tokens, depth), bf16),
            pltpu.VMEM((2 * tokens, 4 * odepth), bf16),
            pltpu.VMEM((4, odepth, width), bf16),
            pltpu.VMEM((2, depth, width), bf16),
            pltpu.VMEM((2, 1, seqs), jnp.int32),
            pltpu.VMEM((2 * tokens, width), f32),
            pltpu.VMEM((2 * tokens, width), f32),
            pltpu.VMEM((2 * nx, 1, LANES), f32),
            pltpu.VMEM((ny, 1, LANES), f32),
            pltpu.VMEM((nz, 1, LANES), f32),
            dma((6,)),
            dma, dma,
            dma((6,)), dma((6,)),
            dma((CHUNKS,)), dma((CHUNKS,)),
            dma((2 * nx,)), dma((2 * nx,)),
            dma((ny,)), dma((ny,)),
            dma((nz,)), dma((nz,)),
        ],
        compiler_params=pltpu.CompilerParams(collective_id=0, has_side_effects=True),
    )(activations, gradients, input_factor, output_factor, lengths.reshape(1, seqs))


def solution(mesh):
    in_specs = (
        P("layer", "dp", None),
        P("layer", "dp", None),
        P("layer", "dp", None),
        P("layer", "dp", None),
        P("dp"),
    )
    out_specs = P("dp", None)
    return jax.shard_map(shards, mesh=mesh, in_specs=in_specs, out_specs=out_specs, check_vma=False)
```

time: 835 us -> 64.9 us (0.08)
  the two profiles are of different devices: /device:TPU:128 before, /device:TPU:1 now
where the time goes in v1:
time: 64.9 us; the launch traced here: 64.7 us
  Pallas kernels  63.5 us (98%)
  local copies, waits for them, and re-layouts  1.26 us (2%)
    pallas_call x1, Pallas kernels, shards(): pl.pallas_call(functools.partial(kernel, dims, blocks), out_shape=jax.Sha...  63.5 us

profile of v1, /device:TPU:1, one launch (start us, length us, event | category | flops | bytes accessed | tf_op | source)
XLA Modules:
  0.0 64.7 jit_solution(16884127511472190404)
XLA Ops:
  0.0 63.5 %shard_map.55 = f32[4,8]{1,0:T(4,128)} custom-call(bf16[1,128,8192]{2,1,0:T(8,128)(2,1)} %act.1, bf16[1,128,896]{2,1,0:T(8,128)(2,1)} %grad.1, bf16[1,2048,256]{2,1,0:T(8,128)(2,1)} %inf.1, bf16[1,224,256]{2,1,0:T(8,128)(2,1)} %outf.1, s32[1,4]{1,0:T(1,128)} %bitcast.1), custom_call_target="tpu_custom_call" | custom-call | tf_op jit(solution)/shard_map/pallas_call | solution.py:197
  63.5 1.3 %copy.7 = f32[4,8]{1,0:T(4,128)} copy(f32[4,8]{1,0:T(4,128)} %shard_map.55) | data formatting | bytes 256

commit v2 on v1

--- a/solution.py
+++ b/solution.py
@@ -15,13 +15,14 @@
 MESH = pl.DeviceIdType.MESH
 LAYER_DIMS = {256: (8, 4, 8), 8: (2, 2, 2), 4: (2, 1, 2)}
 CHUNKS = 8
+ROUNDS = 3
 
 
 def kernel(
     dims, blocks, act, grad, inf, outf, lens, out,
     act_v, grad_v, of_v, if_v, len_v, pi, po, rx1, rx2, rx3,
     local_sem, out_send, out_recv, core_send, core_recv, if_send, if_recv,
-    send1, recv1, send2, recv2, send3, recv3,
+    rounds, send1, recv1, send2, recv2, send3, recv3,
 ):
     ny, nz, nx = dims
     layer, dp = lax.axis_index("layer"), lax.axis_index("dp")
@@ -39,7 +40,10 @@
     def at(y_, z_, x_):
         return (y_ * nz + z_) * nx + x_
 
-    first = [(d, o) for o in (0, 1) for d in range(nx) if d or o]
+    def far_first(n):
+        return sorted(range(1, n), key=lambda d: -min(d, n - d))
+
+    first = [(d, o) for d in far_first(nx) for o in (0, 1)] + [(0, 1)]
 
     def peer1(d, o):
         c = core if o == 0 else 1 - core
@@ -51,18 +55,45 @@
     def peer3(d):
         return {"layer": at(y, lax.rem(z + d, nz), x), "dp": dp}
 
+    def remote(src, dst, send, recv, device):
+        return pltpu.make_async_remote_copy(
+            src_ref=src, dst_ref=dst, send_sem=send, recv_sem=recv, device_id=device, device_id_type=MESH
+        )
+
+    over = {"layer": layer, "dp": cross}
+    beside = {"layer": layer, "dp": partner}
+
     barrier = pltpu.get_barrier_semaphore()
-    peers = [{"layer": layer, "dp": cross}]
-    peers += [peer1(d, o) for d, o in first]
-    peers += [peer2(d) for d in range(1, ny)]
-    peers += [peer3(d) for d in range(1, nz)]
-    for peer in peers:
+    next_z = {"layer": at(y, lax.rem(z + 2 * chip + nz - 1, nz), x), "dp": cross}
+    near = [over, next_z, peer1(1, 0), peer1(nx - 1, 0), peer2(1), peer2(ny - 1)]
+    for peer in [*near, beside]:
         pl.semaphore_signal(barrier, inc=1, device_id=peer, device_id_type=MESH)
+    pl.semaphore_wait(barrier, len(near) + 1)
+
+    out_over = remote(outf.at[0], of_v.at[dp], out_send, out_recv, over)
+    out_over.start()
+
+    def chunk(i):
+        rows = pl.ds(pl.multiple_of(i * step, 16), step)
+        return remote(inf.at[0, rows, :], if_v.at[1, rows, :], if_send.at[i], if_recv.at[i], over)
+
+    for i in range(CHUNKS):
+        chunk(i).start()
 
     def columns(shard):
         return pl.ds(pl.multiple_of(shard * depth, LANES), depth)
 
     mine = pl.ds(pl.multiple_of(core * tokens, 128), tokens)
+    partner_cross = (1 - chip) * 2 + 1 - core
+    swaps = [
+        remote(lens, len_v.at[core], core_send.at[0], core_recv.at[0], beside),
+        remote(outf.at[0], of_v.at[dp], core_send.at[1], core_recv.at[1], beside),
+        remote(grad.at[0], grad_v.at[mine, :], core_send.at[2], core_recv.at[2], beside),
+        remote(act.at[0, :, columns(partner)], act_v.at[0, mine, :], core_send.at[3], core_recv.at[3], beside),
+        remote(act.at[0, :, columns(partner_cross)], act_v.at[1, mine, :], core_send.at[4], core_recv.at[4], beside),
+    ]
+    for copy in swaps:
+        copy.start()
     local = [
         pltpu.make_async_copy(act.at[0, :, columns(dp)], act_v.at[0, mine, :], local_sem.at[0]),
         pltpu.make_async_copy(act.at[0, :, columns(cross)], act_v.at[1, mine, :], local_sem.at[1]),
@@ -73,35 +104,13 @@
     ]
     for copy in local:
         copy.start()
-    pl.semaphore_wait(barrier, len(peers))
-
-    def remote(src, dst, send, recv, device):
-        return pltpu.make_async_remote_copy(
-            src_ref=src, dst_ref=dst, send_sem=send, recv_sem=recv, device_id=device, device_id_type=MESH
-        )
-
-    over = {"layer": layer, "dp": cross}
-    beside = {"layer": layer, "dp": partner}
-    out_over = remote(outf.at[0], of_v.at[dp], out_send, out_recv, over)
-    out_over.start()
-
-    def chunk(i):
-        rows = pl.ds(pl.multiple_of(i * step, 16), step)
-        return remote(inf.at[0, rows, :], if_v.at[1, rows, :], if_send.at[i], if_recv.at[i], over)
-
-    for i in range(CHUNKS):
-        chunk(i).start()
-
-    partner_cross = (1 - chip) * 2 + 1 - core
-    swaps = [
-        remote(lens, len_v.at[core], core_send.at[0], core_recv.at[0], beside),
-        remote(outf.at[0], of_v.at[dp], core_send.at[1], core_recv.at[1], beside),
-        remote(grad.at[0], grad_v.at[mine, :], core_send.at[2], core_recv.at[2], beside),
-        remote(act.at[0, :, columns(partner)], act_v.at[0, mine, :], core_send.at[3], core_recv.at[3], beside),
-        remote(act.at[0, :, columns(partner_cross)], act_v.at[1, mine, :], core_send.at[4], core_recv.at[4], beside),
-    ]
-    for copy in swaps:
-        copy.start()
+    for r in range(ROUNDS):
+        for peer in near:
+            pl.semaphore_signal(rounds.at[r], inc=1, device_id=peer, device_id_type=MESH)
+        pl.semaphore_wait(rounds.at[r], len(near))
+    pl.semaphore_signal(rounds.at[ROUNDS], inc=1, device_id=beside, device_id_type=MESH)
+    pl.semaphore_wait(rounds.at[ROUNDS], 1)
+
     relay = remote(of_v.at[cross], of_v.at[cross], core_send.at[5], core_recv.at[5], beside)
 
     for copy in local:
@@ -113,7 +122,7 @@
         def body(i, carry):
             rows = pl.ds(pl.multiple_of(i * step, LANES), step)
             if block == 1:
-                chunk(i).wait()
+                chunk(i).wait_recv()
             product = jnp.dot(act_v[block, :, rows], if_v[block, rows, :], preferred_element_type=jnp.float32)
             if block == 0:
                 pi[...] = jnp.where(i == 0, product, pi[...] + product)
@@ -146,12 +155,19 @@
 
     width = QUERIES * RANK
     lanes = lax.broadcasted_iota(jnp.int32, (width, LANES), 1)
-    fold = (lax.broadcasted_iota(jnp.int32, (width, LANES), 0) // RANK == lanes % QUERIES).astype(jnp.float32)
+    fold = (lax.broadcasted_iota(jnp.int32, (width, LANES), 0) // RANK == lanes % QUERIES).astype(jnp.bfloat16)
     score = jnp.sum((po[...] * pi[...]).reshape(2 * seqs, SLOT, width), axis=1)
-    score = jnp.dot(score, fold, precision=lax.Precision.HIGHEST, preferred_element_type=jnp.float32)
+    high = score.astype(jnp.bfloat16).astype(jnp.float32)
+    middle = (score - high).astype(jnp.bfloat16).astype(jnp.float32)
+    parts = jnp.concatenate([high, middle, score - high - middle], axis=0).astype(jnp.bfloat16)
+    score = jnp.sum(
+        jnp.dot(parts, fold, preferred_element_type=jnp.float32).reshape(3, 2 * seqs, LANES), axis=0
+    )
     spot = lax.broadcasted_iota(jnp.int32, (2 * seqs, LANES), 1) // QUERIES
     keep = spot == lax.broadcasted_iota(jnp.int32, (2 * seqs, LANES), 0)
     value = jnp.sum(jnp.where(keep, score, 0.0), axis=0, keepdims=True)
+
+    waiting = [chunk(i) for i in range(CHUNKS)]
 
     def exchange(value, rx, me, sends):
         rx[me] = value
@@ -159,7 +175,8 @@
         for copy in copies:
             copy.start()
         for copy in copies:
-            copy.wait()
+            copy.wait_recv()
+        waiting.extend(copies)
         result = rx[0]
         for j in range(1, rx.shape[0]):
             result = result + rx[j]
@@ -175,12 +192,11 @@
     own = lax.broadcasted_iota(jnp.int32, (8, LANES), 0) + core * seqs
     lane = lax.broadcasted_iota(jnp.int32, (8, LANES), 1)
     spread = jnp.where(lane // QUERIES == own, jnp.broadcast_to(value, (8, LANES)), 0.0)
-    gather = (
-        lax.broadcasted_iota(jnp.int32, (LANES, LANES), 0) % QUERIES
-        == lax.broadcasted_iota(jnp.int32, (LANES, LANES), 1)
-    ).astype(jnp.float32)
-    final = jnp.dot(spread, gather, precision=lax.Precision.HIGHEST, preferred_element_type=jnp.float32)
-    out[...] = final[:seqs, :QUERIES] / jnp.float32(math.sqrt(RANK * SLOT * blocks))
+    for shift in (8, 16, 32, 64):
+        spread += pltpu.roll(spread, shift, 1)
+    out[...] = spread[:seqs, :QUERIES] * jnp.float32(1 / math.sqrt(RANK * SLOT * blocks))
+    for copy in waiting:
+        copy.wait_send()
 
 
 def shards(activations, gradients, input_factor, output_factor, lengths):
@@ -214,11 +230,12 @@
             dma, dma,
             dma((6,)), dma((6,)),
             dma((CHUNKS,)), dma((CHUNKS,)),
+            pltpu.SemaphoreType.REGULAR((ROUNDS + 1,)),
             dma((2 * nx,)), dma((2 * nx,)),
             dma((ny,)), dma((ny,)),
             dma((nz,)), dma((nz,)),
         ],
-        compiler_params=pltpu.CompilerParams(collective_id=0, has_side_effects=True),
+        compiler_params=pltpu.CompilerParams(collective_id=0, has_side_effects=True, vmem_limit_bytes=56500000),
     )(activations, gradients, input_factor, output_factor, lengths.reshape(1, seqs))
 
 

time: 64.9 us -> 63.1 us (0.972)
  Pallas kernels: 63.5 us -> 61.3 us
    pallas_call x1, Pallas kernels: 63.5 us -> 61.3 us  [shards(): pl.pallas_call(functools.partial(kernel, dims, blocks), out_shape=jax.Sha...]
where the time goes in v2:
time: 63.1 us; the launch traced here: 62.5 us
  Pallas kernels  61.3 us (97%)
  local copies, waits for them, and re-layouts  1.24 us (2%)
    pallas_call x1, Pallas kernels, shards(): pl.pallas_call(functools.partial(kernel, dims, blocks), out_shape=jax.Sha...  61.3 us

profile of v2, /device:TPU:1, one launch (start us, length us, event | category | flops | bytes accessed | tf_op | source)
XLA Modules:
  0.0 62.5 jit_solution(10504652307618837368)
XLA Ops:
  0.0 0.0 copy-start
  0.0 0.7 %copy-done = s32[4]{0:T(128)S(1)} copy-done((s32[4]{0:T(128)S(1)}, s32[4]{0:T(128)}, u32[]{:S(2)}) %copy-start) | copy-done | bytes 40
  0.7 61.3 %shard_map.55 = f32[4,8]{1,0:T(4,128)S(1)} custom-call(bf16[1,128,8192]{2,1,0:T(8,128)(2,1)} %act.1, bf16[1,128,896]{2,1,0:T(8,128)(2,1)} %grad.1, bf16[1,2048,256]{2,1,0:T(8,128)(2,1)} %inf.1, bf16[1,224,256]{2,1,0:T(8,128)(2,1)} %outf.1, s32[1,4]{1,0:T(1,128)S(1)} %bitcast.1), custom_call_target="tpu_custom_call" | custom-call | tf_op jit(solution)/shard_map/pallas_call | solution.py:213
  62.0 0.6 copy.7
Async XLA Ops:
  0.0 0.7 %copy-start = (s32[4]{0:T(128)S(1)}, s32[4]{0:T(128)}, u32[]{:S(2)}) copy-start(s32[4]{0:T(128)} %param.9) | copy-start | bytes 52

commit v3 on v2

--- a/solution.py
+++ b/solution.py
@@ -15,14 +15,14 @@
 MESH = pl.DeviceIdType.MESH
 LAYER_DIMS = {256: (8, 4, 8), 8: (2, 2, 2), 4: (2, 1, 2)}
 CHUNKS = 8
-ROUNDS = 3
+ROUNDS = 7
 
 
 def kernel(
     dims, blocks, act, grad, inf, outf, lens, out,
-    act_v, grad_v, of_v, if_v, len_v, pi, po, rx1, rx2, rx3,
+    act_v, grad_v, of_v, if_v, len_v, pi, po, rx1, rx2,
     local_sem, out_send, out_recv, core_send, core_recv, if_send, if_recv,
-    rounds, send1, recv1, send2, recv2, send3, recv3,
+    rounds, send1, recv1, send2, recv2,
 ):
     ny, nz, nx = dims
     layer, dp = lax.axis_index("layer"), lax.axis_index("dp")
@@ -49,11 +49,11 @@
         c = core if o == 0 else 1 - core
         return {"layer": at(y, z, lax.rem(x + d, nx)), "dp": chip * 2 + c}
 
-    def peer2(d):
-        return {"layer": at(lax.rem(y + d, ny), z, x), "dp": dp}
-
-    def peer3(d):
-        return {"layer": at(y, lax.rem(z + d, nz), x), "dp": dp}
+    second = [(d, e) for d in range(ny) for e in range(nz) if d or e]
+    second.sort(key=lambda t: -min(t[0], ny - t[0]) - 2 * min(t[1], nz - t[1]))
+
+    def peer2(d, e):
+        return {"layer": at(lax.rem(y + d, ny), lax.rem(z + e, nz), x), "dp": dp}
 
     def remote(src, dst, send, recv, device):
         return pltpu.make_async_remote_copy(
@@ -65,7 +65,7 @@
 
     barrier = pltpu.get_barrier_semaphore()
     next_z = {"layer": at(y, lax.rem(z + 2 * chip + nz - 1, nz), x), "dp": cross}
-    near = [over, next_z, peer1(1, 0), peer1(nx - 1, 0), peer2(1), peer2(ny - 1)]
+    near = [over, next_z, peer1(1, 0), peer1(nx - 1, 0), peer2(1, 0), peer2(ny - 1, 0)]
     for peer in [*near, beside]:
         pl.semaphore_signal(barrier, inc=1, device_id=peer, device_id_type=MESH)
     pl.semaphore_wait(barrier, len(near) + 1)
@@ -185,9 +185,9 @@
     value = exchange(
         value, rx1, core * nx + x, [(send1.at[i], recv1.at[i], peer1(d, o)) for i, (d, o) in enumerate(first)]
     )
-    value = exchange(value, rx2, y, [(send2.at[d], recv2.at[d], peer2(d)) for d in range(1, ny)])
-    if nz > 1:
-        value = exchange(value, rx3, z, [(send3.at[d], recv3.at[d], peer3(d)) for d in range(1, nz)])
+    value = exchange(
+        value, rx2, y * nz + z, [(send2.at[i], recv2.at[i], peer2(d, e)) for i, (d, e) in enumerate(second)]
+    )
 
     own = lax.broadcasted_iota(jnp.int32, (8, LANES), 0) + core * seqs
     lane = lax.broadcasted_iota(jnp.int32, (8, LANES), 1)
@@ -210,6 +210,7 @@
     bf16, f32 = jnp.bfloat16, jnp.float32
     dma = pltpu.SemaphoreType.DMA
     anywhere = pl.BlockSpec(memory_space=pl.ANY)
+    inputs = (activations, gradients, input_factor, output_factor, lengths.reshape(1, seqs))
     return pl.pallas_call(
         functools.partial(kernel, dims, blocks),
         out_shape=jax.ShapeDtypeStruct((seqs, QUERIES), f32),
@@ -224,19 +225,17 @@
             pltpu.VMEM((2 * tokens, width), f32),
             pltpu.VMEM((2 * tokens, width), f32),
             pltpu.VMEM((2 * nx, 1, LANES), f32),
-            pltpu.VMEM((ny, 1, LANES), f32),
-            pltpu.VMEM((nz, 1, LANES), f32),
+            pltpu.VMEM((ny * nz, 1, LANES), f32),
             dma((6,)),
             dma, dma,
             dma((6,)), dma((6,)),
             dma((CHUNKS,)), dma((CHUNKS,)),
             pltpu.SemaphoreType.REGULAR((ROUNDS + 1,)),
             dma((2 * nx,)), dma((2 * nx,)),
-            dma((ny,)), dma((ny,)),
-            dma((nz,)), dma((nz,)),
+            dma((ny * nz,)), dma((ny * nz,)),
         ],
-        compiler_params=pltpu.CompilerParams(collective_id=0, has_side_effects=True, vmem_limit_bytes=56500000),
-    )(activations, gradients, input_factor, output_factor, lengths.reshape(1, seqs))
+        compiler_params=pltpu.CompilerParams(collective_id=0, has_side_effects=True, vmem_limit_bytes=32 << 20),
+    )(*[pltpu.with_memory_space_constraint(a, pltpu.HBM) for a in inputs])
 
 
 def solution(mesh):

time: 63.1 us -> 61.3 us (0.971)
  Pallas kernels: 61.3 us -> 60.6 us
  local copies, waits for them, and re-layouts: 1.24 us -> 0.58 us
    pallas_call x1, Pallas kernels: 61.3 us -> 60.6 us  [shards(): pl.pallas_call(functools.partial(kernel, dims, blocks), out_shape=jax.Sha...]
    unnamed x3 -> x1, local copies, waits for them, and re-layouts: 1.24 us -> 0.58 us
where the time goes in v3:
time: 61.3 us; the launch traced here: 61.2 us
  Pallas kernels  60.6 us (99%)
    pallas_call x1, Pallas kernels, shards(): pl.pallas_call(functools.partial(kernel, dims, blocks), out_shape=jax.Sha...  60.6 us

profile of v3, /device:TPU:1, one launch (start us, length us, event | category | flops | bytes accessed | tf_op | source)
XLA Modules:
  0.0 61.2 jit_solution(17124841087686255521)
XLA Ops:
  0.0 60.6 %shard_map.55 = f32[4,8]{1,0:T(4,128)S(1)} custom-call(bf16[1,128,8192]{2,1,0:T(8,128)(2,1)} %act.1, bf16[1,128,896]{2,1,0:T(8,128)(2,1)} %grad.1, bf16[1,2048,256]{2,1,0:T(8,128)(2,1)} %inf.1, bf16[1,224,256]{2,1,0:T(8,128)(2,1)} %outf.1, s32[1,4]{1,0:T(1,128)} %bitcast.1), custom_call_target="tpu_custom_call" | custom-call | tf_op jit(solution)/shard_map/pallas_call | solution.py:214
  60.6 0.6 copy.7

commit v4 on v3

--- a/solution.py
+++ b/solution.py
@@ -130,7 +130,7 @@
                 pi[...] += product
             return carry
 
-        lax.fori_loop(0, CHUNKS, body, 0)
+        lax.fori_loop(0, CHUNKS - block, body, 0)
 
     out_over.wait()
     relay.start()
@@ -156,7 +156,10 @@
     width = QUERIES * RANK
     lanes = lax.broadcasted_iota(jnp.int32, (width, LANES), 1)
     fold = (lax.broadcasted_iota(jnp.int32, (width, LANES), 0) // RANK == lanes % QUERIES).astype(jnp.bfloat16)
-    score = jnp.sum((po[...] * pi[...]).reshape(2 * seqs, SLOT, width), axis=1)
+    tail = pl.ds((CHUNKS - 1) * step, step)
+    chunk(CHUNKS - 1).wait_recv()
+    last = jnp.dot(act_v[1, :, tail], if_v[1, tail, :], preferred_element_type=jnp.float32)
+    score = jnp.sum((po[...] * (pi[...] + last)).reshape(2 * seqs, SLOT, width), axis=1)
     high = score.astype(jnp.bfloat16).astype(jnp.float32)
     middle = (score - high).astype(jnp.bfloat16).astype(jnp.float32)
     parts = jnp.concatenate([high, middle, score - high - middle], axis=0).astype(jnp.bfloat16)
@@ -177,10 +180,10 @@
         for copy in copies:
             copy.wait_recv()
         waiting.extend(copies)
-        result = rx[0]
-        for j in range(1, rx.shape[0]):
-            result = result + rx[j]
-        return result
+        terms = [rx[j] for j in range(rx.shape[0])]
+        while len(terms) > 1:
+            terms = [a + b for a, b in zip(terms[::2], terms[1::2])]
+        return terms[0]
 
     value = exchange(
         value, rx1, core * nx + x, [(send1.at[i], recv1.at[i], peer1(d, o)) for i, (d, o) in enumerate(first)]

time: 61.3 us -> 61.3 us (level)
  no operation moved by 1% of the time
where the time goes in v4:
time: 61.3 us; the launch traced here: 61.2 us
  Pallas kernels  60.6 us (99%)
    pallas_call x1, Pallas kernels, shards(): pl.pallas_call(functools.partial(kernel, dims, blocks), out_shape=jax.Sha...  60.6 us

profile of v4, /device:TPU:1, one launch (start us, length us, event | category | flops | bytes accessed | tf_op | source)
XLA Modules:
  0.0 61.2 jit_solution(16628970710901378803)
XLA Ops:
  0.0 60.6 %shard_map.55 = f32[4,8]{1,0:T(4,128)S(1)} custom-call(bf16[1,128,8192]{2,1,0:T(8,128)(2,1)} %act.1, bf16[1,128,896]{2,1,0:T(8,128)(2,1)} %grad.1, bf16[1,2048,256]{2,1,0:T(8,128)(2,1)} %inf.1, bf16[1,224,256]{2,1,0:T(8,128)(2,1)} %outf.1, s32[1,4]{1,0:T(1,128)} %bitcast.1), custom_call_target="tpu_custom_call" | custom-call | tf_op jit(solution)/shard_map/pallas_call | solution.py:217
  60.6 0.6 copy.7
